TPU v7x, 1024 devices: a whole 8x8x8 slice. The times are simulated.
1024 devices in a mesh: row: 16 (over y_hi, z), col: 64 (over x, y_lo, core).
Axes of the slice: x: 8, y: 8 (y_hi: 2, y_lo: 4; y = y_hi * 4 + y_lo), z: 8, core: 2. Of those that a mesh axis runs over, the one named last changes fastest.
Arguments:
- inputs: bfloat16 [3, 128, 16384], P(None, 'col', 'row'), may hold values from -16 to 16
- weight: float32 [16384, 26624], P('row', 'col'), may hold values from -0.046875 to 0.046875
- upstream: bfloat16 [3, 128, 26624], P(None, 'row', 'col'), may hold values from -16 to 16
Outputs:
- activation: bfloat16 [3, 128, 26624], P(None, 'row', 'col')
- input_grad: bfloat16 [3, 128, 16384], P(None, 'col', 'row')
- weight_grad: float32 [16384, 26624], P('row', 'col')
All inputs are finite; a program needn't handle non-finite values.
Results may differ from a plain program's by a relative error of at most 0.0063.
Values may be sent and summed in bfloat16 or wider, within the bound.
No kernel may reach another device: no remote copies, remote signals or barrier semaphores. Data moves between devices by JAX's collectives and lax.ppermute only.
A program may use at most 32 MiB of HBM per device.

v0:
```python
import math

import jax
import jax.numpy as jnp
from jax import lax
from jax.sharding import PartitionSpec as P


def joined_along(pieces, dim):
    shape = list(pieces.shape[1:])
    shape[dim] *= pieces.shape[0]
    return jnp.moveaxis(pieces, 0, dim).reshape(shape)


def copy_for_each(shard, axis):
    copies = jnp.broadcast_to(shard, (lax.axis_size(axis), *shard.shape))
    return lax.all_to_all(copies, axis, split_axis=0, concat_axis=0, tiled=True)


def gathered_copies(shard, axis, dim):
    return joined_along(copy_for_each(shard, axis), dim)


def in_blocks(shard, dim, peers):
    shape = shard.shape
    pieces = shard.reshape(*shape[:dim], peers, shape[dim] // peers, *shape[dim + 1 :])
    return jnp.moveaxis(pieces, dim, 0)


def summed_on_arrival(shard, axis, dim):
    peers = lax.axis_size(axis)
    pieces = lax.all_to_all(in_blocks(shard, dim, peers), axis, 0, 0, tiled=True)
    return jnp.sum(pieces, axis=0)


def gelu_parts(pre):
    cdf = 0.5 * (1.0 + jax.scipy.special.erf(pre * (1.0 / math.sqrt(2.0))))
    slope = cdf + pre * jnp.exp(-0.5 * pre * pre) * (1.0 / math.sqrt(2.0 * math.pi))
    return (pre * cdf, slope)


def body(inputs, weight, upstream):
    low = weight.astype(jnp.bfloat16)
    gathered = gathered_copies(inputs, "col", 1)
    partial_value = jnp.einsum("mtd,df->mtf", gathered, low, preferred_element_type=jnp.float32)
    pre = summed_on_arrival(partial_value, "row", 1)
    act, slope = gelu_parts(pre)
    gated = (upstream.astype(jnp.float32) * slope).astype(jnp.bfloat16)
    gathered, acts, gated = (gathered, act.astype(jnp.bfloat16), gated)
    piece = gathered_copies(gated, "row", 1)
    grad_part = jnp.einsum("mtd,mtf->df", gathered, piece, preferred_element_type=jnp.float32)
    term = jnp.einsum("mtf,df->mtd", piece, low, preferred_element_type=jnp.float32)
    dx_part = term
    dx_part, backward_grad = (dx_part, grad_part)
    input_grad = summed_on_arrival(dx_part, "col", 1).astype(jnp.bfloat16)
    grad = backward_grad
    tokens_all = inputs.shape[0] * inputs.shape[1] * lax.axis_size("col")
    grad = grad * (1.0 / math.sqrt(tokens_all))
    return (acts, input_grad, grad)


def solution(mesh):
    placed = (P(None, "col", "row"), P("row", "col"), P(None, "row", "col"))
    return jax.shard_map(
        body,
        mesh=mesh,
        in_specs=placed,
        out_specs=(P(None, "row", "col"), P(None, "col", "row"), P("row", "col")),
        check_vma=False,
    )
```

profile of v0, /device:TPU:1, one launch (start us, length us, event | category | flops | bytes accessed | tf_op | source)
XLA Modules:
  0.0 158.4 jit_solution(2445210422890012582)
XLA Ops:
  0.6 1.1 broadcast_in_dim.6
  1.7 40.5 %all_to_all.20 = bf16[64,3,2,1024]{3,2,1,0:T(2,128)(2,1)S(1)} all-to-all(bf16[64,3,2,1024]{3,2,1,0:T(2,128)(2,1)S(1)} %broadcast_in_dim.6), channel_id=1, replica_groups=mesh['row'=16,'col'=64] {'col'}, dimensions={0} | all-to-all | bytes 1572864 | tf_op jit(solution)/shard_map/all_to_all | solution.py:17
  42.3 0.0 copy-start
  42.3 0.5 copy.9
  42.8 0.3 dot_general.13
  43.1 0.6 copy-done
  43.7 0.6 convolution_bitcast_fusion.1
  44.3 0.0 copy-start.1
  44.3 0.1 copy.10
  44.4 32.3 %all_to_all.21 = f32[16,3,8,416]{3,2,1,0:T(8,128)S(1)} all-to-all(f32[16,3,8,416]{3,2,1,0:T(8,128)S(1)} %copy.10), channel_id=1, replica_groups=mesh['row'=16,'col'=64] {'row'}, dimensions={0} | all-to-all | bytes 1277952 | tf_op jit(solution)/shard_map/all_to_all | solution.py:32
  76.7 0.1 reduce_sum.18
  76.7 0.0 copy-done.1
  76.7 0.6 fusion.12
  77.4 24.2 %all_to_all.22 = bf16[16,3,8,416]{3,2,1,0:T(8,128)(2,1)S(1)} all-to-all(bf16[16,3,8,416]{3,2,1,0:T(8,128)(2,1)S(1)} %broadcast_in_dim.7), channel_id=1, replica_groups=mesh['row'=16,'col'=64] {'row'}, dimensions={0} | all-to-all | bytes 638976 | tf_op jit(solution)/shard_map/all_to_all | solution.py:17
  101.6 0.8 copy.11
  102.4 1.2 dot_general.15
  103.5 0.6 convolution_bitcast_fusion
  104.1 2.4 %copy.13 = f32[64,3,2,1024]{3,2,1,0:T(2,128)} copy(f32[64,3,2,1024]{3,0,2,1:T(8,128)S(1)} %convolution_bitcast_fusion) | data formatting | bytes 3145728 | tf_op jit(solution)/shard_map/transpose | solution.py:27
  106.5 11.1 %all-to-all-start.3 = ((f32[64,3,2,1024]{3,2,1,0:T(2,128)}), f32[64,3,2,1024]{3,2,1,0:T(2,128)S(1)}, u32[]{:S(2)}, u32[]{:S(2)}) async-start(f32[64,3,2,1024]{3,2,1,0:T(2,128)} %copy.13), calls=%async_computation.3 | async-start | bytes 3145728 | tf_op jit(solution)/shard_map/all_to_all | solution.py:32
  117.6 1.2 reshape.19
  118.8 2.9 %fusion = f32[1024,416]{0,1:T(8,128)} fusion(bf16[3,128,1024]{2,1,0:T(8,128)(2,1)} %reshape.19, bf16[16,3,8,416]{3,2,1,0:T(8,128)(2,1)S(1)} %all_to_all.22), kind=kOutput, calls=%fused_computation.1 | convolution fusion | flops 327581696 | bytes 2809856 | tf_op jit(solution)/shard_map/mtd,mtf->df/dot_general | solution.py:51
  121.7 35.5 %all-to-all-done.3 = f32[64,3,2,1024]{3,2,1,0:T(2,128)S(1)} async-done(((f32[64,3,2,1024]{3,2,1,0:T(2,128)}), f32[64,3,2,1024]{3,2,1,0:T(2,128)S(1)}, u32[]{:S(2)}, u32[]{:S(2)}) %all-to-all-start.3) | async-done | bytes 1572896 | tf_op jit(solution)/shard_map/all_to_all | solution.py:32
  157.2 1.2 reduce_sum.19
  (1 shorter events, 0.0 us)
Async XLA Ops:
  42.3 1.5 copy-start
  44.3 32.4 %copy-start.1 = (bf16[3,8,416]{2,1,0:T(8,128)(2,1)S(1)}, bf16[3,8,416]{2,1,0:T(8,128)(2,1)}, u32[]{:S(2)}) copy-start(bf16[3,8,416]{2,1,0:T(8,128)(2,1)} %param.5) | copy-start | bytes 59908
  106.5 50.8 %all-to-all-start.3 = ((f32[64,3,2,1024]{3,2,1,0:T(2,128)}), f32[64,3,2,1024]{3,2,1,0:T(2,128)S(1)}, u32[]{:S(2)}, u32[]{:S(2)}) async-start(f32[64,3,2,1024]{3,2,1,0:T(2,128)} %copy.13), calls=%async_computation.3 | async-start | bytes 3145728 | tf_op jit(solution)/shard_map/all_to_all | solution.py:32
where the time goes:
time: 159 us; the launch traced here: 158 us
  blocking collectives  97 us (61%)
  waiting for transfers between devices  35.5 us (22%)
  starting transfers between devices  11.1 us (7%)
  local copies, waits for them, and re-layouts  8.14 us (5%)
  matrix products  4.1 us (3%)
  other arithmetic  1.84 us (1%)
    all_to_all x2, blocking collectives, copy_for_each(): return lax.all_to_all(copies, axis, split_axis=0, concat_axis=0, tiled=True)  64.7 us
    all_to_all x1, waiting for transfers between devices, summed_on_arrival(): lax.all_to_all(in_blocks(shard, dim, peers), axis, 0, 0, tiled=True)  35.5 us
    all_to_all x1, blocking collectives, summed_on_arrival(): lax.all_to_all(in_blocks(shard, dim, peers), axis, 0, 0, tiled=True)  32.3 us
    all_to_all x1, starting transfers between devices, summed_on_arrival(): lax.all_to_all(in_blocks(shard, dim, peers), axis, 0, 0, tiled=True)  11.1 us
  transfers between devices with their start and end apart: 1, of which 1 were waited for; matrix products, arithmetic and copies ran while one was open for 3% of the time, Pallas kernels for 0%

commit v1 on v0

v1 whole, which is shorter than its diff:
```python
import math

import jax
import jax.numpy as jnp
from jax import lax
from jax.sharding import Mesh, PartitionSpec as P

BF = jnp.bfloat16
F32 = jnp.float32
SWAP = [(0, 1), (1, 0)]


def gelu_parts(pre):
    cdf = 0.5 * (1.0 + jax.scipy.special.erf(pre * (1.0 / math.sqrt(2.0))))
    slope = cdf + pre * jnp.exp(-0.5 * pre * pre) * (1.0 / math.sqrt(2.0 * math.pi))
    return (pre * cdf, slope)


def copy_for_each(shard, axis):
    copies = jnp.broadcast_to(shard, (lax.axis_size(axis), *shard.shape))
    return lax.all_to_all(copies, axis, split_axis=0, concat_axis=0, tiled=True)


def exchange(pieces, axis):
    return lax.all_to_all(pieces, axis, split_axis=0, concat_axis=0, tiled=True)


def body(inputs, weight, upstream):
    micro, own, width = inputs.shape
    hidden = weight.shape[1]
    rows, chips = lax.axis_size("row"), lax.axis_size("chip")
    tokens = upstream.shape[1]
    me = lax.axis_index("core")
    total = chips * micro * own
    mine = total // rows
    spare = -(2 * hidden) % 128

    low = weight.T.astype(BF)
    split = upstream.reshape(micro, tokens // (2 * own), 2, own, hidden)
    split = jnp.moveaxis(split, 2, 0).transpose(0, 2, 1, 3, 4).reshape(2, mine, hidden)
    kept = lax.dynamic_index_in_dim(split, me, 0, keepdims=False)
    given = lax.dynamic_index_in_dim(split, 1 - me, 0, keepdims=False)
    other_low = lax.ppermute(low, "core", SWAP)
    other_up = lax.ppermute(given, "core", SWAP)
    both = jnp.concatenate([low, other_low, jnp.zeros((spare, width), BF)], 0)
    up = jnp.concatenate([kept, other_up, jnp.zeros((mine, spare), BF)], 1)

    x = copy_for_each(inputs, "chip").reshape(total, width)
    part = lax.dot_general(x, both, (((1,), (1,)), ((), ())), preferred_element_type=F32)
    part = part.astype(BF).reshape(rows, mine // 4, 4, -1)
    pieces = exchange(part, "row").reshape(rows, mine, -1)
    other_x = lax.ppermute(x, "core", SWAP)

    act, slope = gelu_parts(jnp.sum(pieces.astype(F32), axis=0))
    gated = (up.astype(F32) * slope).astype(BF)
    act = act.astype(BF)
    gathered = copy_for_each(gated.reshape(mine // 4, 4, -1), "row").reshape(total, -1)

    term = lax.dot_general(gathered, both, (((1,), (0,)), ((), ())), preferred_element_type=F32)
    dx = exchange(term.astype(BF).reshape(chips, micro, own, width), "chip")

    other_gated = lax.ppermute(gathered[:, hidden : 2 * hidden], "core", SWAP)
    other_act = lax.ppermute(act[:, hidden : 2 * hidden], "core", SWAP)
    xs = jnp.concatenate([x, other_x], 0)
    gs = jnp.concatenate([gathered[:, :hidden], other_gated], 0)
    grad = lax.dot_general(xs, gs, (((0,), (0,)), ((), ())), preferred_element_type=F32)
    grad = grad * (1.0 / math.sqrt(2 * total))

    shape = (tokens // (2 * own), micro, own, hidden)
    held, got = act[:, :hidden].reshape(shape), other_act.reshape(shape)
    acts = jnp.stack([jnp.where(me == 0, held, got), jnp.where(me == 0, got, held)], 2)
    acts = jnp.moveaxis(acts, 0, 1).reshape(micro, tokens, hidden)
    input_grad = jnp.sum(dx.astype(F32), axis=0).astype(BF)
    return (acts, input_grad, grad)


def solution(mesh):
    rows, cols = mesh.devices.shape
    fine = Mesh(mesh.devices.reshape(rows, cols // 2, 2), ("row", "chip", "core"))
    col = ("chip", "core")
    placed = (P(None, col, "row"), P("row", col), P(None, "row", col))
    return jax.shard_map(
        body,
        mesh=fine,
        in_specs=placed,
        out_specs=(P(None, "row", col), P(None, col, "row"), P("row", col)),
        check_vma=False,
    )
```

time: 159 us -> 112 us (0.70)
  the two profiles are of different devices: /device:TPU:1 before, /device:TPU:2 now
where the time goes in v1:
time: 112 us; the launch traced here: 111 us
  starting transfers between devices  52.7 us (47%)
  waiting for transfers between devices  45.2 us (40%)
  local copies, waits for them, and re-layouts  4.9 us (4%)
  matrix products  4.39 us (4%)
  other arithmetic  2.82 us (3%)
    all_to_all x2, waiting for transfers between devices, copy_for_each(): return lax.all_to_all(copies, axis, split_axis=0, concat_axis=0, tiled=True)  28.6 us
    all_to_all x2, starting transfers between devices, copy_for_each(): return lax.all_to_all(copies, axis, split_axis=0, concat_axis=0, tiled=True)  21.8 us
    all_to_all x2, starting transfers between devices, exchange(): return lax.all_to_all(pieces, axis, split_axis=0, concat_axis=0, tiled=True)  20.9 us
    all_to_all x2, waiting for transfers between devices, exchange(): return lax.all_to_all(pieces, axis, split_axis=0, concat_axis=0, tiled=True)  15.2 us
    dot_general x1, matrix products, body(): lax.dot_general(xs, gs, (((0,), (0,)), ((), ())), preferred_element_type=...  2.84 us
    ppermute x1, starting transfers between devices, body(): other_gated = lax.ppermute(gathered[:, hidden:2 * hidden], 'core', SWAP)  2.41 us
  transfers between devices with their start and end apart: 9, of which 6 were waited for; matrix products, arithmetic and copies ran while one was open for 6% of the time, Pallas kernels for 0%

profile of v1, /device:TPU:2, one launch (start us, length us, event | category | flops | bytes accessed | tf_op | source)
XLA Modules:
  0.0 111.0 jit_solution(5604971150369064129)
XLA Ops:
  0.6 1.6 %convert_bitcast_fusion = bf16[416,1024]{1,0:T(8,128)(2,1)S(1)} fusion(f32[1024,416]{0,1:T(8,128)} %param.4), kind=kLoop, calls=%fused_computation.7 | loop fusion | flops 425984 | bytes 2555904 | tf_op jit(solution)/shard_map/convert_element_type | solution.py:38
  2.2 1.9 %collective-permute-start = (bf16[416,1024]{1,0:T(8,128)(2,1)S(1)}, bf16[416,1024]{1,0:T(8,128)(2,1)S(1)}, u32[]{:S(2)}, u32[]{:S(2)}) collective-permute-start(bf16[416,1024]{1,0:T(8,128)(2,1)S(1)} %convert_bitcast_fusion), channel_id=1, source_target_pairs={{0,1},{1,0},{2,3},{3,2},{4,5},{5,4},{6,7},{7,6},{8,9},{9,8},{10,11... | collective-permute-start | bytes 2555912 | tf_op jit(solution)/shard_map/ppermute | solution.py:43
  4.2 1.0 broadcast_in_dim.13
  5.1 16.7 %all-to-all-start = ((bf16[32,3,2,1024]{3,2,1,0:T(2,128)(2,1)}), bf16[32,3,2,1024]{3,2,1,0:T(2,128)(2,1)S(1)}, u32[]{:S(2)}, u32[]{:S(2)}) async-start(bf16[32,3,2,1024]{3,2,1,0:T(2,128)(2,1)} %broadcast_in_dim.13), calls=%async_computation | async-start | bytes 786432 | tf_op jit(solution)/shard_map/all_to_all | solution.py:21
  21.9 16.2 %all-to-all-done = bf16[32,3,2,1024]{3,2,1,0:T(2,128)(2,1)S(1)} async-done(((bf16[32,3,2,1024]{3,2,1,0:T(2,128)(2,1)}), bf16[32,3,2,1024]{3,2,1,0:T(2,128)(2,1)S(1)}, u32[]{:S(2)}, u32[]{:S(2)}) %all-to-all-start) | async-done | bytes 393248 | tf_op jit(solution)/shard_map/all_to_all | solution.py:21
  38.2 0.1 reshape.76
  38.3 0.9 fusion
  39.2 0.8 reshape.77
  40.0 13.5 %all-to-all-start.1 = ((bf16[16,3,4,896]{3,2,1,0:T(4,128)(2,1)}), bf16[16,3,4,896]{3,2,1,0:T(4,128)(2,1)S(1)}, u32[]{:S(2)}, u32[]{:S(2)}) async-start(bf16[16,3,4,896]{3,2,1,0:T(4,128)(2,1)} %reshape.77), calls=%async_computation.1 | async-start | bytes 688128 | tf_op jit(solution)/shard_map/all_to_all | solution.py:25
  53.6 0.1 dynamic-slice_reduce_fusion
  53.7 1.9 %collective-permute-start.2 = (bf16[12,416]{1,0:T(8,128)(2,1)S(1)}, bf16[12,416]{1,0:T(8,128)(2,1)S(1)}, u32[]{:S(2)}, u32[]{:S(2)}) collective-permute-start(bf16[12,416]{1,0:T(8,128)(2,1)S(1)} %bitcast.15), channel_id=1, source_target_pairs={{0,1},{1,0},{2,3},{3,2},{4,5},{5,4},{6,7},{7,6},{8,9},{9,8},{10,11... | collective-permute-start | bytes 29960 | tf_op jit(solution)/shard_map/ppermute | solution.py:44
  55.6 1.1 %collective-permute-done.2 = bf16[12,416]{1,0:T(8,128)(2,1)S(1)} collective-permute-done((bf16[12,416]{1,0:T(8,128)(2,1)S(1)}, bf16[12,416]{1,0:T(8,128)(2,1)S(1)}, u32[]{:S(2)}, u32[]{:S(2)}) %collective-permute-start.2) | collective-permute-done | bytes 10016 | tf_op jit(solution)/shard_map/ppermute | solution.py:44
  56.8 10.4 %all-to-all-done.1 = bf16[16,3,4,896]{3,2,1,0:T(4,128)(2,1)S(1)} async-done(((bf16[16,3,4,896]{3,2,1,0:T(4,128)(2,1)}), bf16[16,3,4,896]{3,2,1,0:T(4,128)(2,1)S(1)}, u32[]{:S(2)}, u32[]{:S(2)}) %all-to-all-start.1) | async-done | bytes 344096 | tf_op jit(solution)/shard_map/all_to_all | solution.py:25
  67.2 0.1 convert_reduce_fusion
  67.4 0.1 fusion.14
  67.5 0.8 broadcast_in_dim.15
  68.3 5.1 %all-to-all-start.2 = ((bf16[16,3,4,896]{3,2,1,0:T(4,128)(2,1)}), bf16[16,3,4,896]{3,2,1,0:T(4,128)(2,1)S(1)}, u32[]{:S(2)}, u32[]{:S(2)}) async-start(bf16[16,3,4,896]{3,2,1,0:T(4,128)(2,1)} %broadcast_in_dim.15), calls=%async_computation.2 | async-start | bytes 688128 | tf_op jit(solution)/shard_map/all_to_all | solution.py:21
  73.4 1.9 %collective-permute-start.3 = (bf16[192,1024]{1,0:T(8,128)(2,1)S(1)}, bf16[192,1024]{1,0:T(8,128)(2,1)}, u32[]{:S(2)}, u32[]{:S(2)}) collective-permute-start(bf16[192,1024]{1,0:T(8,128)(2,1)S(1)} %reshape.76), channel_id=1, source_target_pairs={{0,1},{1,0},{2,3},{3,2},{4,5},{5,4},{6,7},{7,6},{8,9},{9,8},{10,11... | collective-permute-start | bytes 1179656 | tf_op jit(solution)/shard_map/ppermute | solution.py:52
  75.3 12.4 %all-to-all-done.2 = bf16[16,3,4,896]{3,2,1,0:T(4,128)(2,1)S(1)} async-done(((bf16[16,3,4,896]{3,2,1,0:T(4,128)(2,1)}), bf16[16,3,4,896]{3,2,1,0:T(4,128)(2,1)S(1)}, u32[]{:S(2)}, u32[]{:S(2)}) %all-to-all-start.2) | async-done | bytes 344096 | tf_op jit(solution)/shard_map/all_to_all | solution.py:21
  87.7 0.1 reshape.81
  87.8 0.7 convolution_convert_fusion
  88.5 0.9 reshape.82
  89.4 7.4 %all-to-all-start.3 = ((bf16[32,3,2,1024]{3,2,1,0:T(2,128)(2,1)}), bf16[32,3,2,1024]{3,2,1,0:T(2,128)(2,1)S(1)}, u32[]{:S(2)}, u32[]{:S(2)}) async-start(bf16[32,3,2,1024]{3,2,1,0:T(2,128)(2,1)} %reshape.82), calls=%async_computation.3 | async-start | bytes 786432 | tf_op jit(solution)/shard_map/all_to_all | solution.py:25
  96.9 0.1 slice.17
  97.0 1.9 %collective-permute-start.1 = (bf16[12,416]{1,0:T(8,128)(2,1)S(1)}, bf16[12,416]{1,0:T(8,128)(2,1)S(1)}, u32[]{:S(2)}, u32[]{:S(2)}) collective-permute-start(bf16[12,416]{1,0:T(8,128)(2,1)S(1)} %slice.17), channel_id=1, source_target_pairs={{0,1},{1,0},{2,3},{3,2},{4,5},{5,4},{6,7},{7,6},{8,9},{9,8},{10,11... | collective-permute-start | bytes 29960 | tf_op jit(solution)/shard_map/ppermute | solution.py:63
  98.9 0.1 fusion.18
  99.0 2.4 %collective-permute-start.4 = (bf16[192,416]{1,0:T(8,128)(2,1)S(1)}, bf16[192,416]{1,0:T(8,128)(2,1)S(1)}, u32[]{:S(2)}, u32[]{:S(2)}) collective-permute-start(bf16[192,416]{1,0:T(8,128)(2,1)S(1)} %get-tuple-element.4), channel_id=1, source_target_pairs={{0,1},{1,0},{2,3},{3,2},{4,5},{5,4},{6,7},{7,6},{8,9},{9,8},{10,11... | collective-permute-start | bytes 479240 | tf_op jit(solution)/shard_map/ppermute | solution.py:62
  101.6 0.6 reshape.78
  102.2 0.3 collective-permute-done.4
  102.5 2.8 %convolution_multiply_fusion = f32[1024,416]{0,1:T(8,128)} fusion(bf16[192,1024]{1,0:T(8,128)(2,1)} %collective-permute-done.3, bf16[192,1024]{1,0:T(8,128)(2,1)S(1)} %reshape.76, bf16[192,416]{1,0:T(8,128)(2,1)S(1)} %collective-permute-done.4, bf16[192,416]{1,0:T(8,128)(2,1)S(1)} %get-tuple-element.3), kind=kOutput, calls=%fused_computation.1 | convolution fusion | flops 329793536 | bytes 2809856 | tf_op jit(solution)/shard_map/dot_general | solution.py:66
  105.3 4.7 %all-to-all-done.3 = bf16[32,3,2,1024]{3,2,1,0:T(2,128)(2,1)S(1)} async-done(((bf16[32,3,2,1024]{3,2,1,0:T(2,128)(2,1)}), bf16[32,3,2,1024]{3,2,1,0:T(2,128)(2,1)S(1)}, u32[]{:S(2)}, u32[]{:S(2)}) %all-to-all-start.3) | async-done | bytes 393248 | tf_op jit(solution)/shard_map/all_to_all | solution.py:25
  110.0 0.9 reduce_sum.25
  (21 shorter events, 0.3 us)
Async XLA Ops:
  0.6 3.5 %copy-start.1 = (bf16[3,2,1024]{2,1,0:T(2,128)(2,1)S(1)}, bf16[3,2,1024]{2,1,0:T(2,128)(2,1)}, u32[]{:S(2)}) copy-start(bf16[3,2,1024]{2,1,0:T(2,128)(2,1)} %param.3) | copy-start | bytes 36868
  2.2 36.1 %collective-permute-start = (bf16[416,1024]{1,0:T(8,128)(2,1)S(1)}, bf16[416,1024]{1,0:T(8,128)(2,1)S(1)}, u32[]{:S(2)}, u32[]{:S(2)}) collective-permute-start(bf16[416,1024]{1,0:T(8,128)(2,1)S(1)} %convert_bitcast_fusion), channel_id=1, source_target_pairs={{0,1},{1,0},{2,3},{3,2},{4,5},{5,4},{6,7},{7,6},{8,9},{9,8},{10,11... | collective-permute-start | bytes 2555912 | tf_op jit(solution)/shard_map/ppermute | solution.py:43
  5.1 33.0 %all-to-all-start = ((bf16[32,3,2,1024]{3,2,1,0:T(2,128)(2,1)}), bf16[32,3,2,1024]{3,2,1,0:T(2,128)(2,1)S(1)}, u32[]{:S(2)}, u32[]{:S(2)}) async-start(bf16[32,3,2,1024]{3,2,1,0:T(2,128)(2,1)} %broadcast_in_dim.13), calls=%async_computation | async-start | bytes 786432 | tf_op jit(solution)/shard_map/all_to_all | solution.py:21
  38.3 15.2 %copy-start = (bf16[3,8,416]{2,1,0:T(8,128)(2,1)S(1)}, bf16[3,8,416]{2,1,0:T(8,128)(2,1)}, u32[]{:S(2)}) copy-start(bf16[3,8,416]{2,1,0:T(8,128)(2,1)} %param.5) | copy-start | bytes 59908
  40.0 27.2 %all-to-all-start.1 = ((bf16[16,3,4,896]{3,2,1,0:T(4,128)(2,1)}), bf16[16,3,4,896]{3,2,1,0:T(4,128)(2,1)S(1)}, u32[]{:S(2)}, u32[]{:S(2)}) async-start(bf16[16,3,4,896]{3,2,1,0:T(4,128)(2,1)} %reshape.77), calls=%async_computation.1 | async-start | bytes 688128 | tf_op jit(solution)/shard_map/all_to_all | solution.py:25
  53.7 3.1 %collective-permute-start.2 = (bf16[12,416]{1,0:T(8,128)(2,1)S(1)}, bf16[12,416]{1,0:T(8,128)(2,1)S(1)}, u32[]{:S(2)}, u32[]{:S(2)}) collective-permute-start(bf16[12,416]{1,0:T(8,128)(2,1)S(1)} %bitcast.15), channel_id=1, source_target_pairs={{0,1},{1,0},{2,3},{3,2},{4,5},{5,4},{6,7},{7,6},{8,9},{9,8},{10,11... | collective-permute-start | bytes 29960 | tf_op jit(solution)/shard_map/ppermute | solution.py:44
  68.3 19.5 %all-to-all-start.2 = ((bf16[16,3,4,896]{3,2,1,0:T(4,128)(2,1)}), bf16[16,3,4,896]{3,2,1,0:T(4,128)(2,1)S(1)}, u32[]{:S(2)}, u32[]{:S(2)}) async-start(bf16[16,3,4,896]{3,2,1,0:T(4,128)(2,1)} %broadcast_in_dim.15), calls=%async_computation.2 | async-start | bytes 688128 | tf_op jit(solution)/shard_map/all_to_all | solution.py:21
  73.4 28.8 %collective-permute-start.3 = (bf16[192,1024]{1,0:T(8,128)(2,1)S(1)}, bf16[192,1024]{1,0:T(8,128)(2,1)}, u32[]{:S(2)}, u32[]{:S(2)}) collective-permute-start(bf16[192,1024]{1,0:T(8,128)(2,1)S(1)} %reshape.76), channel_id=1, source_target_pairs={{0,1},{1,0},{2,3},{3,2},{4,5},{5,4},{6,7},{7,6},{8,9},{9,8},{10,11... | collective-permute-start | bytes 1179656 | tf_op jit(solution)/shard_map/ppermute | solution.py:52
  89.4 20.6 %all-to-all-start.3 = ((bf16[32,3,2,1024]{3,2,1,0:T(2,128)(2,1)}), bf16[32,3,2,1024]{3,2,1,0:T(2,128)(2,1)S(1)}, u32[]{:S(2)}, u32[]{:S(2)}) async-start(bf16[32,3,2,1024]{3,2,1,0:T(2,128)(2,1)} %reshape.82), calls=%async_computation.3 | async-start | bytes 786432 | tf_op jit(solution)/shard_map/all_to_all | solution.py:25
  97.0 4.5 %collective-permute-start.1 = (bf16[12,416]{1,0:T(8,128)(2,1)S(1)}, bf16[12,416]{1,0:T(8,128)(2,1)S(1)}, u32[]{:S(2)}, u32[]{:S(2)}) collective-permute-start(bf16[12,416]{1,0:T(8,128)(2,1)S(1)} %slice.17), channel_id=1, source_target_pairs={{0,1},{1,0},{2,3},{3,2},{4,5},{5,4},{6,7},{7,6},{8,9},{9,8},{10,11... | collective-permute-start | bytes 29960 | tf_op jit(solution)/shard_map/ppermute | solution.py:63
  99.0 3.5 %collective-permute-start.4 = (bf16[192,416]{1,0:T(8,128)(2,1)S(1)}, bf16[192,416]{1,0:T(8,128)(2,1)S(1)}, u32[]{:S(2)}, u32[]{:S(2)}) collective-permute-start(bf16[192,416]{1,0:T(8,128)(2,1)S(1)} %get-tuple-element.4), channel_id=1, source_target_pairs={{0,1},{1,0},{2,3},{3,2},{4,5},{5,4},{6,7},{7,6},{8,9},{9,8},{10,11... | collective-permute-start | bytes 479240 | tf_op jit(solution)/shard_map/ppermute | solution.py:62

commit v2 on v1

v2 whole, which is shorter than its diff:
```python
import math

import jax
import jax.numpy as jnp
from jax import lax
from jax.sharding import Mesh, PartitionSpec as P


BF = jnp.bfloat16
F32 = jnp.float32
SWAP = [(0, 1), (1, 0)]
AXES = ("yh", "z", "xh", "xl", "y1", "y0", "core")
ROW = ("yh", "z")
COL = ("xh", "xl", "y1", "y0", "core")
CHIP = ("xl", "y1", "xh", "y0")


def exchange(pieces, axis):
    return lax.all_to_all(pieces, axis, split_axis=0, concat_axis=0, tiled=True)


def copy_for_each(shard, axis):
    return exchange(jnp.broadcast_to(shard, (lax.axis_size(axis), *shard.shape)), axis)


def swapped(value, axis="core"):
    return lax.ppermute(value, axis, SWAP)


def body(inputs, weight, upstream):
    micro, own, width = inputs.shape
    hidden = weight.shape[1]
    depth, chips = lax.axis_size("z"), lax.axis_size(CHIP)
    tokens = upstream.shape[1]
    core, half = lax.axis_index("core"), lax.axis_index("yh")
    total = chips * micro * own
    mine = total // (2 * depth)
    spare = -(2 * hidden) % 128

    x = copy_for_each(inputs, CHIP)
    x = x.reshape(total, width)

    low = weight.T.astype(BF)
    both = jnp.concatenate([low, swapped(low), jnp.zeros((spare, width), BF)], 0)
    split = upstream.reshape(micro, tokens // (2 * own), 2, own, hidden)
    split = split.transpose(2, 1, 0, 3, 4).reshape(2, mine, hidden)
    kept = jnp.where(core == 0, split[0], split[1])
    given = jnp.where(core == 0, split[1], split[0])
    up = jnp.concatenate([kept, swapped(given), jnp.zeros((mine, spare), BF)], 1)
    far = swapped(up, "yh")
    up = jnp.concatenate([jnp.where(half == 0, up, far), jnp.where(half == 0, far, up)], 0)

    part = lax.dot_general(x, both, (((1,), (1,)), ((), ())), preferred_element_type=F32)
    pieces = exchange(part.astype(BF).reshape(depth, 2 * mine, -1), "z")
    partial = jnp.sum(pieces.astype(F32), axis=0).astype(BF)
    other = swapped(partial, "yh")
    other_x = swapped(x)
    pre = partial.astype(F32) + other.astype(F32)

    cdf = 0.5 * (1.0 + jax.scipy.special.erf(pre * (1.0 / math.sqrt(2.0))))
    slope = cdf + pre * jnp.exp(-0.5 * pre * pre) * (1.0 / math.sqrt(2.0 * math.pi))
    gated = (up.astype(F32) * slope).astype(BF)
    gathered = copy_for_each(gated, "z").reshape(total, -1)

    term = lax.dot_general(gathered, both, (((1,), (0,)), ((), ())), preferred_element_type=F32)
    dx = exchange(term.astype(BF).reshape(chips, micro, own, width), CHIP)
    act = pre * cdf
    act = jnp.where(half == 0, act[:mine], act[mine:]).astype(BF)
    other_act = swapped(act[:, hidden : 2 * hidden])

    other_gated = swapped(gathered[:, hidden : 2 * hidden])
    xs = jnp.concatenate([x, other_x], 0)
    gs = jnp.concatenate([gathered[:, :hidden], other_gated], 0)
    grad = lax.dot_general(xs, gs, (((0,), (0,)), ((), ())), preferred_element_type=F32)
    grad = grad * (1.0 / math.sqrt(2 * total))

    shape = (tokens // (2 * own), micro, own, hidden)
    held, got = act[:, :hidden].reshape(shape), other_act.reshape(shape)
    acts = jnp.stack([jnp.where(core == 0, held, got), jnp.where(core == 0, got, held)], 2)
    acts = jnp.moveaxis(acts, 0, 1).reshape(micro, tokens, hidden)
    input_grad = jnp.sum(dx.astype(F32), axis=0).astype(BF)
    return (acts, input_grad, grad)


def solution(mesh):
    fine = Mesh(mesh.devices.reshape(2, 8, 2, 4, 2, 2, 2), AXES)
    return jax.shard_map(
        body,
        mesh=fine,
        in_specs=(P(None, COL, ROW), P(ROW, COL), P(None, ROW, COL)),
        out_specs=(P(None, ROW, COL), P(None, COL, ROW), P(ROW, COL)),
        check_vma=False,
    )
```

time: 112 us -> 109 us (0.973)
  the two profiles are of different devices: /device:TPU:2 before, /device:TPU:18 now
where the time goes in v2:
time: 109 us
  starting transfers between devices  56.4 us (52%)
  waiting for transfers between devices  40.5 us (37%)
  matrix products  4.1 us (4%)
  local copies, waits for them, and re-layouts  3.82 us (4%)
  other arithmetic  2.85 us (3%)
    all_to_all x4, starting transfers between devices, exchange(): return lax.all_to_all(pieces, axis, split_axis=0, concat_axis=0, tiled=True)  35.4 us
    all_to_all x4, waiting for transfers between devices, exchange(): return lax.all_to_all(pieces, axis, split_axis=0, concat_axis=0, tiled=True)  34.8 us
    ppermute x7, starting transfers between devices, swapped(): return lax.ppermute(value, axis, SWAP)  21 us
    ppermute x7, waiting for transfers between devices, swapped(): return lax.ppermute(value, axis, SWAP)  5.69 us
  transfers between devices with their start and end apart: 11, of which 7 were waited for; matrix products, arithmetic and copies ran while one was open for 5% of the time, Pallas kernels for 0%

profile of v2, /device:TPU:18, one launch (start us, length us, event | category | flops | bytes accessed | tf_op | source)
XLA Modules:
  0.0 108.6 jit_solution(1621103859451995188)
XLA Ops:
  0.6 1.6 %convert_bitcast_fusion = bf16[416,1024]{1,0:T(8,128)(2,1)S(1)} fusion(f32[1024,416]{0,1:T(8,128)} %param.4), kind=kLoop, calls=%fused_computation.6 | loop fusion | flops 425984 | bytes 2555904 | tf_op jit(solution)/shard_map/convert_element_type | solution.py:43
  2.2 1.9 %collective-permute-start = (bf16[416,1024]{1,0:T(8,128)(2,1)S(1)}, bf16[416,1024]{1,0:T(8,128)(2,1)S(1)}, u32[]{:S(2)}, u32[]{:S(2)}) collective-permute-start(bf16[416,1024]{1,0:T(8,128)(2,1)S(1)} %convert_bitcast_fusion), channel_id=1, source_target_pairs={{0,1},{1,0},{2,3},{3,2},{4,5},{5,4},{6,7},{7,6},{8,9},{9,8},{10,11... | collective-permute-start | bytes 2555912 | tf_op jit(solution)/shard_map/ppermute | solution.py:27
  4.2 1.0 broadcast_in_dim.13
  5.1 16.5 %all-to-all-start = ((bf16[32,3,2,1024]{3,2,1,0:T(2,128)(2,1)}), bf16[32,3,2,1024]{3,2,1,0:T(2,128)(2,1)S(1)}, u32[]{:S(2)}, u32[]{:S(2)}) async-start(bf16[32,3,2,1024]{3,2,1,0:T(2,128)(2,1)} %broadcast_in_dim.13), calls=%async_computation | async-start | bytes 786432 | tf_op jit(solution)/shard_map/all_to_all | solution.py:19
  21.7 0.1 pad.13.clone
  21.7 15.8 %all-to-all-done = bf16[32,3,2,1024]{3,2,1,0:T(2,128)(2,1)S(1)} async-done(((bf16[32,3,2,1024]{3,2,1,0:T(2,128)(2,1)}), bf16[32,3,2,1024]{3,2,1,0:T(2,128)(2,1)S(1)}, u32[]{:S(2)}, u32[]{:S(2)}) %all-to-all-start) | async-done | bytes 393248 | tf_op jit(solution)/shard_map/all_to_all | solution.py:19
  37.5 0.1 reshape.73
  37.7 1.6 %convolution_convert_fusion.1 = bf16[896,192]{0,1:T(8,128)(2,1)} fusion(bf16[192,1024]{1,0:T(8,128)(2,1)S(1)} %reshape.73, bf16[416,1024]{1,0:T(8,128)(2,1)S(1)} %collective-permute-done, bf16[416,1024]{1,0:T(8,128)(2,1)S(1)} %convert_bitcast_fusion, bf16[896]{0:T(1024)(128)(2,1)S(1)} %pad.13.clone), kind=kOutput, calls=%fused_computation.3 | convolution fusion | flops 357998592 | bytes 2443008 | tf_op jit(solution)/shard_map/dot_general | solution.py:53
  39.3 10.3 %all-to-all-start.1 = ((bf16[8,24,896]{2,1,0:T(8,128)(2,1)}), bf16[8,24,896]{2,1,0:T(8,128)(2,1)S(1)}, u32[]{:S(2)}, u32[]{:S(2)}) async-start(bf16[8,24,896]{2,1,0:T(8,128)(2,1)} %bitcast.2), calls=%async_computation.1 | async-start | bytes 688128 | tf_op jit(solution)/shard_map/all_to_all | solution.py:19
  49.8 1.9 %collective-permute-start.3 = (bf16[12,416]{1,0:T(8,128)(2,1)S(1)}, bf16[12,416]{1,0:T(8,128)(2,1)S(1)}, u32[]{:S(2)}, u32[]{:S(2)}) collective-permute-start(bf16[12,416]{1,0:T(8,128)(2,1)S(1)} %select_n.79), channel_id=1, source_target_pairs={{0,1},{1,0},{2,3},{3,2},{4,5},{5,4},{6,7},{7,6},{8,9},{9,8},{10,11... | collective-permute-start | bytes 29960 | tf_op jit(solution)/shard_map/ppermute | solution.py:27
  51.7 1.1 %collective-permute-done.3 = bf16[12,416]{1,0:T(8,128)(2,1)S(1)} collective-permute-done((bf16[12,416]{1,0:T(8,128)(2,1)S(1)}, bf16[12,416]{1,0:T(8,128)(2,1)S(1)}, u32[]{:S(2)}, u32[]{:S(2)}) %collective-permute-start.3) | collective-permute-done | bytes 10016 | tf_op jit(solution)/shard_map/ppermute | solution.py:27
  52.8 0.1 maximum_maximum_fusion.3
  52.9 5.5 %collective-permute-start.4 = (bf16[12,896]{1,0:T(8,128)(2,1)S(1)}, bf16[12,896]{1,0:T(8,128)(2,1)S(1)}, u32[]{:S(2)}, u32[]{:S(2)}) collective-permute-start(bf16[12,896]{1,0:T(8,128)(2,1)S(1)} %maximum_maximum_fusion.3), channel_id=1, source_target_pairs={{0,512},{512,0},{1,513},{513,1},{2,514},{514,2},{3,515},{515,3},{4... | collective-permute-start | bytes 64520 | tf_op jit(solution)/shard_map/ppermute | solution.py:27
  58.4 3.5 %all-to-all-done.1 = bf16[8,24,896]{2,1,0:T(8,128)(2,1)S(1)} async-done(((bf16[8,24,896]{2,1,0:T(8,128)(2,1)}), bf16[8,24,896]{2,1,0:T(8,128)(2,1)S(1)}, u32[]{:S(2)}, u32[]{:S(2)}) %all-to-all-start.1) | async-done | bytes 344096 | tf_op jit(solution)/shard_map/all_to_all | solution.py:19
  61.9 5.5 %collective-permute-start.1 = (bf16[24,896]{1,0:T(8,128)(2,1)S(1)}, bf16[24,896]{1,0:T(8,128)(2,1)S(1)}, u32[]{:S(2)}, u32[]{:S(2)}) collective-permute-start(bf16[24,896]{1,0:T(8,128)(2,1)S(1)} %reduce_sum.24), channel_id=1, source_target_pairs={{0,512},{512,0},{1,513},{513,1},{2,514},{514,2},{3,515},{515,3},{4... | collective-permute-start | bytes 129032 | tf_op jit(solution)/shard_map/ppermute | solution.py:27
  67.5 4.3 %collective-permute-done.1 = bf16[24,896]{1,0:T(8,128)(2,1)S(1)} collective-permute-done((bf16[24,896]{1,0:T(8,128)(2,1)S(1)}, bf16[24,896]{1,0:T(8,128)(2,1)S(1)}, u32[]{:S(2)}, u32[]{:S(2)}) %collective-permute-start.1) | collective-permute-done | bytes 43040 | tf_op jit(solution)/shard_map/ppermute | solution.py:27
  71.8 0.8 broadcast_in_dim.15
  72.6 4.2 %all-to-all-start.2 = ((bf16[8,24,896]{2,1,0:T(8,128)(2,1)}), bf16[8,24,896]{2,1,0:T(8,128)(2,1)S(1)}, u32[]{:S(2)}, u32[]{:S(2)}) async-start(bf16[8,24,896]{2,1,0:T(8,128)(2,1)} %broadcast_in_dim.15), calls=%async_computation.2 | async-start | bytes 688128 | tf_op jit(solution)/shard_map/all_to_all | solution.py:19
  76.8 1.9 %collective-permute-start.5 = (bf16[192,1024]{1,0:T(8,128)(2,1)S(1)}, bf16[192,1024]{1,0:T(8,128)(2,1)S(1)}, u32[]{:S(2)}, u32[]{:S(2)}) collective-permute-start(bf16[192,1024]{1,0:T(8,128)(2,1)S(1)} %reshape.73), channel_id=1, source_target_pairs={{0,1},{1,0},{2,3},{3,2},{4,5},{5,4},{6,7},{7,6},{8,9},{9,8},{10,11... | collective-permute-start | bytes 1179656 | tf_op jit(solution)/shard_map/ppermute | solution.py:27
  78.7 10.6 %all-to-all-done.2 = bf16[8,24,896]{2,1,0:T(8,128)(2,1)S(1)} async-done(((bf16[8,24,896]{2,1,0:T(8,128)(2,1)}), bf16[8,24,896]{2,1,0:T(8,128)(2,1)S(1)}, u32[]{:S(2)}, u32[]{:S(2)}) %all-to-all-start.2) | async-done | bytes 344096 | tf_op jit(solution)/shard_map/all_to_all | solution.py:19
  89.3 0.7 convolution_convert_fusion
  90.0 0.9 reshape.78
  90.9 4.4 %all-to-all-start.3 = ((bf16[32,3,2,1024]{3,2,1,0:T(2,128)(2,1)}), bf16[32,3,2,1024]{3,2,1,0:T(2,128)(2,1)S(1)}, u32[]{:S(2)}, u32[]{:S(2)}) async-start(bf16[32,3,2,1024]{3,2,1,0:T(2,128)(2,1)} %reshape.78), calls=%async_computation.3 | async-start | bytes 786432 | tf_op jit(solution)/shard_map/all_to_all | solution.py:19
  95.3 0.1 slice.39
  95.4 1.9 %collective-permute-start.2 = (bf16[12,416]{1,0:T(8,128)(2,1)S(1)}, bf16[12,416]{1,0:T(8,128)(2,1)S(1)}, u32[]{:S(2)}, u32[]{:S(2)}) collective-permute-start(bf16[12,416]{1,0:T(8,128)(2,1)S(1)} %slice.39), channel_id=1, source_target_pairs={{0,1},{1,0},{2,3},{3,2},{4,5},{5,4},{6,7},{7,6},{8,9},{9,8},{10,11... | collective-permute-start | bytes 29960 | tf_op jit(solution)/shard_map/ppermute | solution.py:27
  97.3 0.1 fusion.19
  97.4 2.4 %collective-permute-start.6 = (bf16[192,416]{1,0:T(8,128)(2,1)S(1)}, bf16[192,416]{1,0:T(8,128)(2,1)S(1)}, u32[]{:S(2)}, u32[]{:S(2)}) collective-permute-start(bf16[192,416]{1,0:T(8,128)(2,1)S(1)} %get-tuple-element.4), channel_id=1, source_target_pairs={{0,1},{1,0},{2,3},{3,2},{4,5},{5,4},{6,7},{7,6},{8,9},{9,8},{10,11... | collective-permute-start | bytes 479240 | tf_op jit(solution)/shard_map/ppermute | solution.py:27
  100.0 0.6 reshape.75
  100.6 0.3 collective-permute-done.6
  100.9 1.8 %convolution_multiply_fusion = f32[1024,416]{0,1:T(8,128)} fusion(bf16[192,1024]{1,0:T(8,128)(2,1)S(1)} %collective-permute-done.5, bf16[192,1024]{1,0:T(8,128)(2,1)S(1)} %reshape.73, bf16[192,416]{1,0:T(8,128)(2,1)S(1)} %collective-permute-done.6, bf16[192,416]{1,0:T(8,128)(2,1)S(1)} %get-tuple-element.3), kind=kOutput, calls=%fused_computation.1 | convolution fusion | flops 329793536 | bytes 2809856 | tf_op jit(solution)/shard_map/dot_general | solution.py:74
  102.7 5.0 %all-to-all-done.3 = bf16[32,3,2,1024]{3,2,1,0:T(2,128)(2,1)S(1)} async-done(((bf16[32,3,2,1024]{3,2,1,0:T(2,128)(2,1)}), bf16[32,3,2,1024]{3,2,1,0:T(2,128)(2,1)S(1)}, u32[]{:S(2)}, u32[]{:S(2)}) %all-to-all-start.3) | async-done | bytes 393248 | tf_op jit(solution)/shard_map/all_to_all | solution.py:19
  107.7 0.9 reduce_sum.25
  (24 shorter events, 0.4 us)
Async XLA Ops:
  0.6 3.5 %copy-start.1 = (bf16[3,2,1024]{2,1,0:T(2,128)(2,1)S(1)}, bf16[3,2,1024]{2,1,0:T(2,128)(2,1)}, u32[]{:S(2)}) copy-start(bf16[3,2,1024]{2,1,0:T(2,128)(2,1)} %param.3) | copy-start | bytes 36868
  2.2 35.5 %collective-permute-start = (bf16[416,1024]{1,0:T(8,128)(2,1)S(1)}, bf16[416,1024]{1,0:T(8,128)(2,1)S(1)}, u32[]{:S(2)}, u32[]{:S(2)}) collective-permute-start(bf16[416,1024]{1,0:T(8,128)(2,1)S(1)} %convert_bitcast_fusion), channel_id=1, source_target_pairs={{0,1},{1,0},{2,3},{3,2},{4,5},{5,4},{6,7},{7,6},{8,9},{9,8},{10,11... | collective-permute-start | bytes 2555912 | tf_op jit(solution)/shard_map/ppermute | solution.py:27
  5.1 32.4 %all-to-all-start = ((bf16[32,3,2,1024]{3,2,1,0:T(2,128)(2,1)}), bf16[32,3,2,1024]{3,2,1,0:T(2,128)(2,1)S(1)}, u32[]{:S(2)}, u32[]{:S(2)}) async-start(bf16[32,3,2,1024]{3,2,1,0:T(2,128)(2,1)} %broadcast_in_dim.13), calls=%async_computation | async-start | bytes 786432 | tf_op jit(solution)/shard_map/all_to_all | solution.py:19
  37.7 11.9 %copy-start = (bf16[3,8,416]{2,1,0:T(8,128)(2,1)S(1)}, bf16[3,8,416]{2,1,0:T(8,128)(2,1)}, u32[]{:S(2)}) copy-start(bf16[3,8,416]{2,1,0:T(8,128)(2,1)} %param.5) | copy-start | bytes 59908
  39.3 22.6 %all-to-all-start.1 = ((bf16[8,24,896]{2,1,0:T(8,128)(2,1)}), bf16[8,24,896]{2,1,0:T(8,128)(2,1)S(1)}, u32[]{:S(2)}, u32[]{:S(2)}) async-start(bf16[8,24,896]{2,1,0:T(8,128)(2,1)} %bitcast.2), calls=%async_computation.1 | async-start | bytes 688128 | tf_op jit(solution)/shard_map/all_to_all | solution.py:19
  49.8 3.1 %collective-permute-start.3 = (bf16[12,416]{1,0:T(8,128)(2,1)S(1)}, bf16[12,416]{1,0:T(8,128)(2,1)S(1)}, u32[]{:S(2)}, u32[]{:S(2)}) collective-permute-start(bf16[12,416]{1,0:T(8,128)(2,1)S(1)} %select_n.79), channel_id=1, source_target_pairs={{0,1},{1,0},{2,3},{3,2},{4,5},{5,4},{6,7},{7,6},{8,9},{9,8},{10,11... | collective-permute-start | bytes 29960 | tf_op jit(solution)/shard_map/ppermute | solution.py:27
  52.9 14.5 %collective-permute-start.4 = (bf16[12,896]{1,0:T(8,128)(2,1)S(1)}, bf16[12,896]{1,0:T(8,128)(2,1)S(1)}, u32[]{:S(2)}, u32[]{:S(2)}) collective-permute-start(bf16[12,896]{1,0:T(8,128)(2,1)S(1)} %maximum_maximum_fusion.3), channel_id=1, source_target_pairs={{0,512},{512,0},{1,513},{513,1},{2,514},{514,2},{3,515},{515,3},{4... | collective-permute-start | bytes 64520 | tf_op jit(solution)/shard_map/ppermute | solution.py:27
  61.9 9.8 %collective-permute-start.1 = (bf16[24,896]{1,0:T(8,128)(2,1)S(1)}, bf16[24,896]{1,0:T(8,128)(2,1)S(1)}, u32[]{:S(2)}, u32[]{:S(2)}) collective-permute-start(bf16[24,896]{1,0:T(8,128)(2,1)S(1)} %reduce_sum.24), channel_id=1, source_target_pairs={{0,512},{512,0},{1,513},{513,1},{2,514},{514,2},{3,515},{515,3},{4... | collective-permute-start | bytes 129032 | tf_op jit(solution)/shard_map/ppermute | solution.py:27
  72.6 16.7 %all-to-all-start.2 = ((bf16[8,24,896]{2,1,0:T(8,128)(2,1)}), bf16[8,24,896]{2,1,0:T(8,128)(2,1)S(1)}, u32[]{:S(2)}, u32[]{:S(2)}) async-start(bf16[8,24,896]{2,1,0:T(8,128)(2,1)} %broadcast_in_dim.15), calls=%async_computation.2 | async-start | bytes 688128 | tf_op jit(solution)/shard_map/all_to_all | solution.py:19
  76.8 23.8 %collective-permute-start.5 = (bf16[192,1024]{1,0:T(8,128)(2,1)S(1)}, bf16[192,1024]{1,0:T(8,128)(2,1)S(1)}, u32[]{:S(2)}, u32[]{:S(2)}) collective-permute-start(bf16[192,1024]{1,0:T(8,128)(2,1)S(1)} %reshape.73), channel_id=1, source_target_pairs={{0,1},{1,0},{2,3},{3,2},{4,5},{5,4},{6,7},{7,6},{8,9},{9,8},{10,11... | collective-permute-start | bytes 1179656 | tf_op jit(solution)/shard_map/ppermute | solution.py:27
  90.9 16.8 %all-to-all-start.3 = ((bf16[32,3,2,1024]{3,2,1,0:T(2,128)(2,1)}), bf16[32,3,2,1024]{3,2,1,0:T(2,128)(2,1)S(1)}, u32[]{:S(2)}, u32[]{:S(2)}) async-start(bf16[32,3,2,1024]{3,2,1,0:T(2,128)(2,1)} %reshape.78), calls=%async_computation.3 | async-start | bytes 786432 | tf_op jit(solution)/shard_map/all_to_all | solution.py:19
  95.4 4.5 %collective-permute-start.2 = (bf16[12,416]{1,0:T(8,128)(2,1)S(1)}, bf16[12,416]{1,0:T(8,128)(2,1)S(1)}, u32[]{:S(2)}, u32[]{:S(2)}) collective-permute-start(bf16[12,416]{1,0:T(8,128)(2,1)S(1)} %slice.39), channel_id=1, source_target_pairs={{0,1},{1,0},{2,3},{3,2},{4,5},{5,4},{6,7},{7,6},{8,9},{9,8},{10,11... | collective-permute-start | bytes 29960 | tf_op jit(solution)/shard_map/ppermute | solution.py:27
  97.4 3.5 %collective-permute-start.6 = (bf16[192,416]{1,0:T(8,128)(2,1)S(1)}, bf16[192,416]{1,0:T(8,128)(2,1)S(1)}, u32[]{:S(2)}, u32[]{:S(2)}) collective-permute-start(bf16[192,416]{1,0:T(8,128)(2,1)S(1)} %get-tuple-element.4), channel_id=1, source_target_pairs={{0,1},{1,0},{2,3},{3,2},{4,5},{5,4},{6,7},{7,6},{8,9},{9,8},{10,11... | collective-permute-start | bytes 479240 | tf_op jit(solution)/shard_map/ppermute | solution.py:27

commit v3 on v2

--- a/solution.py
+++ b/solution.py
@@ -41,21 +41,23 @@
     x = x.reshape(total, width)
 
     low = weight.T.astype(BF)
-    both = jnp.concatenate([low, swapped(low), jnp.zeros((spare, width), BF)], 0)
+    other_low = swapped(low)
+    both = jnp.concatenate([low, other_low, jnp.zeros((spare, width), BF)], 0)
+    both = lax.optimization_barrier(both)
     split = upstream.reshape(micro, tokens // (2 * own), 2, own, hidden)
     split = split.transpose(2, 1, 0, 3, 4).reshape(2, mine, hidden)
     kept = jnp.where(core == 0, split[0], split[1])
     given = jnp.where(core == 0, split[1], split[0])
     up = jnp.concatenate([kept, swapped(given), jnp.zeros((mine, spare), BF)], 1)
-    far = swapped(up, "yh")
-    up = jnp.concatenate([jnp.where(half == 0, up, far), jnp.where(half == 0, far, up)], 0)
 
     part = lax.dot_general(x, both, (((1,), (1,)), ((), ())), preferred_element_type=F32)
     pieces = exchange(part.astype(BF).reshape(depth, 2 * mine, -1), "z")
+    other_x = swapped(x)
     partial = jnp.sum(pieces.astype(F32), axis=0).astype(BF)
-    other = swapped(partial, "yh")
-    other_x = swapped(x)
-    pre = partial.astype(F32) + other.astype(F32)
+    other = swapped(jnp.concatenate([partial, up], 0), "yh")
+    far = other[2 * mine :]
+    pre = partial.astype(F32) + other[: 2 * mine].astype(F32)
+    up = jnp.concatenate([jnp.where(half == 0, up, far), jnp.where(half == 0, far, up)], 0)
 
     cdf = 0.5 * (1.0 + jax.scipy.special.erf(pre * (1.0 / math.sqrt(2.0))))
     slope = cdf + pre * jnp.exp(-0.5 * pre * pre) * (1.0 / math.sqrt(2.0 * math.pi))

time: 109 us -> 112 us (1.028)
  waiting for transfers between devices: 40.5 us -> 46 us
  starting transfers between devices: 56.4 us -> 51.6 us
  local copies, waits for them, and re-layouts: 3.82 us -> 5.22 us
    ppermute x7 -> x6, starting transfers between devices: 21 us -> 15.6 us  [swapped(): return lax.ppermute(value, axis, SWAP)]
    all_to_all x4, waiting for transfers between devices: 34.8 us -> 40.3 us  [exchange(): return lax.all_to_all(pieces, axis, split_axis=0, concat_axis=0, tiled=True)]
    ppermute x7 -> x6, waiting for transfers between devices: 5.69 us -> 5.67 us  [swapped(): return lax.ppermute(value, axis, SWAP)]
  transfers between devices with their start and end apart: 11 -> 10, of which waited for: 7 -> 6; matrix products, arithmetic and copies ran while one was open for 5% -> 6% of each run, Pallas kernels for 0% -> 0%
where the time goes in v3:
time: 112 us; the launch traced here: 111 us
  starting transfers between devices  51.6 us (46%)
  waiting for transfers between devices  46 us (41%)
  local copies, waits for them, and re-layouts  5.22 us (5%)
  matrix products  3.96 us (4%)
  other arithmetic  3.27 us (3%)
    all_to_all x4, waiting for transfers between devices, exchange(): return lax.all_to_all(pieces, axis, split_axis=0, concat_axis=0, tiled=True)  40.3 us
    all_to_all x4, starting transfers between devices, exchange(): return lax.all_to_all(pieces, axis, split_axis=0, concat_axis=0, tiled=True)  36 us
    ppermute x6, starting transfers between devices, swapped(): return lax.ppermute(value, axis, SWAP)  15.6 us
    ppermute x6, waiting for transfers between devices, swapped(): return lax.ppermute(value, axis, SWAP)  5.67 us
  transfers between devices with their start and end apart: 10, of which 6 were waited for; matrix products, arithmetic and copies ran while one was open for 6% of the time, Pallas kernels for 0%

profile of v3, /device:TPU:18, one launch (start us, length us, event | category | flops | bytes accessed | tf_op | source)
XLA Modules:
  0.0 110.9 jit_solution(4293757273408787107)
XLA Ops:
  0.6 1.6 %convert_bitcast_fusion = bf16[416,1024]{1,0:T(8,128)(2,1)S(1)} fusion(f32[1024,416]{0,1:T(8,128)} %param.4), kind=kLoop, calls=%fused_computation.4 | loop fusion | flops 425984 | bytes 2555904 | tf_op jit(solution)/shard_map/convert_element_type | solution.py:43
  2.2 1.9 %collective-permute-start = (bf16[416,1024]{1,0:T(8,128)(2,1)S(1)}, bf16[416,1024]{1,0:T(8,128)(2,1)S(1)}, u32[]{:S(2)}, u32[]{:S(2)}) collective-permute-start(bf16[416,1024]{1,0:T(8,128)(2,1)S(1)} %convert_bitcast_fusion), channel_id=1, source_target_pairs={{0,1},{1,0},{2,3},{3,2},{4,5},{5,4},{6,7},{7,6},{8,9},{9,8},{10,11... | collective-permute-start | bytes 2555912 | tf_op jit(solution)/shard_map/ppermute | solution.py:27
  4.2 1.0 broadcast_in_dim.13
  5.1 16.5 %all-to-all-start = ((bf16[32,3,2,1024]{3,2,1,0:T(2,128)(2,1)}), bf16[32,3,2,1024]{3,2,1,0:T(2,128)(2,1)S(1)}, u32[]{:S(2)}, u32[]{:S(2)}) async-start(bf16[32,3,2,1024]{3,2,1,0:T(2,128)(2,1)} %broadcast_in_dim.13), calls=%async_computation | async-start | bytes 786432 | tf_op jit(solution)/shard_map/all_to_all | solution.py:19
  21.7 15.8 %all-to-all-done = bf16[32,3,2,1024]{3,2,1,0:T(2,128)(2,1)S(1)} async-done(((bf16[32,3,2,1024]{3,2,1,0:T(2,128)(2,1)}), bf16[32,3,2,1024]{3,2,1,0:T(2,128)(2,1)S(1)}, u32[]{:S(2)}, u32[]{:S(2)}) %all-to-all-start) | async-done | bytes 393248 | tf_op jit(solution)/shard_map/all_to_all | solution.py:19
  37.5 0.9 reshape.73
  38.4 0.3 maximum_maximum_fusion
  38.8 0.6 copy-done
  39.4 1.5 %convolution_convert_fusion.1 = bf16[896,192]{0,1:T(8,128)(2,1)} fusion(bf16[896,1024]{1,0:T(8,128)(2,1)S(1)} %maximum_maximum_fusion, bf16[192,1024]{1,0:T(8,128)(2,1)S(1)} %copy-done), kind=kOutput, calls=%fused_computation.3 | convolution fusion | flops 352493568 | bytes 2572288 | tf_op jit(solution)/shard_map/dot_general | solution.py:53
  41.0 10.5 %all-to-all-start.1 = ((bf16[8,24,896]{2,1,0:T(8,128)(2,1)}), bf16[8,24,896]{2,1,0:T(8,128)(2,1)S(1)}, u32[]{:S(2)}, u32[]{:S(2)}) async-start(bf16[8,24,896]{2,1,0:T(8,128)(2,1)} %bitcast.2), calls=%async_computation.1 | async-start | bytes 688128 | tf_op jit(solution)/shard_map/all_to_all | solution.py:19
  51.6 1.9 %collective-permute-start.1 = (bf16[12,416]{1,0:T(8,128)(2,1)S(1)}, bf16[12,416]{1,0:T(8,128)(2,1)S(1)}, u32[]{:S(2)}, u32[]{:S(2)}) collective-permute-start(bf16[12,416]{1,0:T(8,128)(2,1)S(1)} %select_n.74), channel_id=1, source_target_pairs={{0,1},{1,0},{2,3},{3,2},{4,5},{5,4},{6,7},{7,6},{8,9},{9,8},{10,11... | collective-permute-start | bytes 29960 | tf_op jit(solution)/shard_map/ppermute | solution.py:27
  53.5 10.2 %all-to-all-done.1 = bf16[8,24,896]{2,1,0:T(8,128)(2,1)S(1)} async-done(((bf16[8,24,896]{2,1,0:T(8,128)(2,1)}), bf16[8,24,896]{2,1,0:T(8,128)(2,1)S(1)}, u32[]{:S(2)}, u32[]{:S(2)}) %all-to-all-start.1) | async-done | bytes 344096 | tf_op jit(solution)/shard_map/all_to_all | solution.py:19
  63.8 0.1 maximum_maximum_fusion.1
  63.8 5.5 %collective-permute-start.2 = (bf16[36,896]{1,0:T(8,128)(2,1)S(1)}, bf16[36,896]{1,0:T(8,128)(2,1)S(1)}, u32[]{:S(2)}, u32[]{:S(2)}) collective-permute-start(bf16[36,896]{1,0:T(8,128)(2,1)S(1)} %maximum_maximum_fusion.1), channel_id=1, source_target_pairs={{0,512},{512,0},{1,513},{513,1},{2,514},{514,2},{3,515},{515,3},{4... | collective-permute-start | bytes 193544 | tf_op jit(solution)/shard_map/ppermute | solution.py:27
  69.3 5.4 %collective-permute-done.2 = bf16[36,896]{1,0:T(8,128)(2,1)S(1)} collective-permute-done((bf16[36,896]{1,0:T(8,128)(2,1)S(1)}, bf16[36,896]{1,0:T(8,128)(2,1)S(1)}, u32[]{:S(2)}, u32[]{:S(2)}) %collective-permute-start.2) | collective-permute-done | bytes 64544 | tf_op jit(solution)/shard_map/ppermute | solution.py:27
  74.7 0.1 broadcast_select_fusion.1
  74.9 0.8 broadcast_in_dim.15
  75.6 3.4 %all-to-all-start.2 = ((bf16[8,24,896]{2,1,0:T(8,128)(2,1)}), bf16[8,24,896]{2,1,0:T(8,128)(2,1)S(1)}, u32[]{:S(2)}, u32[]{:S(2)}) async-start(bf16[8,24,896]{2,1,0:T(8,128)(2,1)} %broadcast_in_dim.15), calls=%async_computation.2 | async-start | bytes 688128 | tf_op jit(solution)/shard_map/all_to_all | solution.py:19
  79.1 1.9 %collective-permute-start.4 = (bf16[192,1024]{1,0:T(8,128)(2,1)S(1)}, bf16[192,1024]{1,0:T(8,128)(2,1)S(1)}, u32[]{:S(2)}, u32[]{:S(2)}) collective-permute-start(bf16[192,1024]{1,0:T(8,128)(2,1)S(1)} %copy-done.1), channel_id=1, source_target_pairs={{0,1},{1,0},{2,3},{3,2},{4,5},{5,4},{6,7},{7,6},{8,9},{9,8},{10,11... | collective-permute-start | bytes 1179656 | tf_op jit(solution)/shard_map/ppermute | solution.py:27
  81.1 9.3 %all-to-all-done.2 = bf16[8,24,896]{2,1,0:T(8,128)(2,1)S(1)} async-done(((bf16[8,24,896]{2,1,0:T(8,128)(2,1)}), bf16[8,24,896]{2,1,0:T(8,128)(2,1)S(1)}, u32[]{:S(2)}, u32[]{:S(2)}) %all-to-all-start.2) | async-done | bytes 344096 | tf_op jit(solution)/shard_map/all_to_all | solution.py:19
  90.4 0.6 convolution_convert_fusion
  90.9 0.9 reshape.78
  91.9 5.6 %all-to-all-start.3 = ((bf16[32,3,2,1024]{3,2,1,0:T(2,128)(2,1)}), bf16[32,3,2,1024]{3,2,1,0:T(2,128)(2,1)S(1)}, u32[]{:S(2)}, u32[]{:S(2)}) async-start(bf16[32,3,2,1024]{3,2,1,0:T(2,128)(2,1)} %reshape.78), calls=%async_computation.3 | async-start | bytes 786432 | tf_op jit(solution)/shard_map/all_to_all | solution.py:19
  97.5 0.1 slice.50
  97.6 1.9 %collective-permute-start.3 = (bf16[12,416]{1,0:T(8,128)(2,1)S(1)}, bf16[12,416]{1,0:T(8,128)(2,1)S(1)}, u32[]{:S(2)}, u32[]{:S(2)}) collective-permute-start(bf16[12,416]{1,0:T(8,128)(2,1)S(1)} %slice.50), channel_id=1, source_target_pairs={{0,1},{1,0},{2,3},{3,2},{4,5},{5,4},{6,7},{7,6},{8,9},{9,8},{10,11... | collective-permute-start | bytes 29960 | tf_op jit(solution)/shard_map/ppermute | solution.py:27
  99.5 0.1 fusion.15
  99.6 2.4 %collective-permute-start.5 = (bf16[192,416]{1,0:T(8,128)(2,1)S(1)}, bf16[192,416]{1,0:T(8,128)(2,1)S(1)}, u32[]{:S(2)}, u32[]{:S(2)}) collective-permute-start(bf16[192,416]{1,0:T(8,128)(2,1)S(1)} %get-tuple-element.4), channel_id=1, source_target_pairs={{0,1},{1,0},{2,3},{3,2},{4,5},{5,4},{6,7},{7,6},{8,9},{9,8},{10,11... | collective-permute-start | bytes 479240 | tf_op jit(solution)/shard_map/ppermute | solution.py:27
  102.2 0.6 reshape.76
  102.8 0.3 collective-permute-done.5
  103.1 1.8 %convolution_multiply_fusion = f32[1024,416]{0,1:T(8,128)} fusion(bf16[192,1024]{1,0:T(8,128)(2,1)S(1)} %collective-permute-done.4, bf16[192,1024]{1,0:T(8,128)(2,1)S(1)} %copy-done.1, bf16[192,416]{1,0:T(8,128)(2,1)S(1)} %collective-permute-done.5, bf16[192,416]{1,0:T(8,128)(2,1)S(1)} %get-tuple-element.3), kind=kOutput, calls=%fused_computation.1 | convolution fusion | flops 329793536 | bytes 2809856 | tf_op jit(solution)/shard_map/dot_general | solution.py:76
  104.9 5.0 %all-to-all-done.3 = bf16[32,3,2,1024]{3,2,1,0:T(2,128)(2,1)S(1)} async-done(((bf16[32,3,2,1024]{3,2,1,0:T(2,128)(2,1)}), bf16[32,3,2,1024]{3,2,1,0:T(2,128)(2,1)S(1)}, u32[]{:S(2)}, u32[]{:S(2)}) %all-to-all-start.3) | async-done | bytes 393248 | tf_op jit(solution)/shard_map/all_to_all | solution.py:19
  109.9 0.9 reduce_sum.25
  (28 shorter events, 0.5 us)
Async XLA Ops:
  0.6 3.5 %copy-start.3 = (bf16[3,2,1024]{2,1,0:T(2,128)(2,1)S(1)}, bf16[3,2,1024]{2,1,0:T(2,128)(2,1)}, u32[]{:S(2)}) copy-start(bf16[3,2,1024]{2,1,0:T(2,128)(2,1)} %param.3) | copy-start | bytes 36868
  2.2 36.2 %collective-permute-start = (bf16[416,1024]{1,0:T(8,128)(2,1)S(1)}, bf16[416,1024]{1,0:T(8,128)(2,1)S(1)}, u32[]{:S(2)}, u32[]{:S(2)}) collective-permute-start(bf16[416,1024]{1,0:T(8,128)(2,1)S(1)} %convert_bitcast_fusion), channel_id=1, source_target_pairs={{0,1},{1,0},{2,3},{3,2},{4,5},{5,4},{6,7},{7,6},{8,9},{9,8},{10,11... | collective-permute-start | bytes 2555912 | tf_op jit(solution)/shard_map/ppermute | solution.py:27
  5.1 32.4 %all-to-all-start = ((bf16[32,3,2,1024]{3,2,1,0:T(2,128)(2,1)}), bf16[32,3,2,1024]{3,2,1,0:T(2,128)(2,1)S(1)}, u32[]{:S(2)}, u32[]{:S(2)}) async-start(bf16[32,3,2,1024]{3,2,1,0:T(2,128)(2,1)} %broadcast_in_dim.13), calls=%async_computation | async-start | bytes 786432 | tf_op jit(solution)/shard_map/all_to_all | solution.py:19
  38.4 1.0 copy-start
  39.4 12.0 %copy-start.2 = (bf16[3,8,416]{2,1,0:T(8,128)(2,1)S(1)}, bf16[3,8,416]{2,1,0:T(8,128)(2,1)}, u32[]{:S(2)}) copy-start(bf16[3,8,416]{2,1,0:T(8,128)(2,1)} %param.5) | copy-start | bytes 59908
  41.0 38.1 %copy-start.1 = (bf16[192,1024]{1,0:T(8,128)(2,1)S(1)}, bf16[192,1024]{1,0:T(8,128)(2,1)}, u32[]{:S(2)}) copy-start(bf16[192,1024]{1,0:T(8,128)(2,1)} %reshape.73) | copy-start | bytes 1179652
  41.0 22.7 %all-to-all-start.1 = ((bf16[8,24,896]{2,1,0:T(8,128)(2,1)}), bf16[8,24,896]{2,1,0:T(8,128)(2,1)S(1)}, u32[]{:S(2)}, u32[]{:S(2)}) async-start(bf16[8,24,896]{2,1,0:T(8,128)(2,1)} %bitcast.2), calls=%async_computation.1 | async-start | bytes 688128 | tf_op jit(solution)/shard_map/all_to_all | solution.py:19
  51.6 12.2 %collective-permute-start.1 = (bf16[12,416]{1,0:T(8,128)(2,1)S(1)}, bf16[12,416]{1,0:T(8,128)(2,1)S(1)}, u32[]{:S(2)}, u32[]{:S(2)}) collective-permute-start(bf16[12,416]{1,0:T(8,128)(2,1)S(1)} %select_n.74), channel_id=1, source_target_pairs={{0,1},{1,0},{2,3},{3,2},{4,5},{5,4},{6,7},{7,6},{8,9},{9,8},{10,11... | collective-permute-start | bytes 29960 | tf_op jit(solution)/shard_map/ppermute | solution.py:27
  63.8 10.9 %collective-permute-start.2 = (bf16[36,896]{1,0:T(8,128)(2,1)S(1)}, bf16[36,896]{1,0:T(8,128)(2,1)S(1)}, u32[]{:S(2)}, u32[]{:S(2)}) collective-permute-start(bf16[36,896]{1,0:T(8,128)(2,1)S(1)} %maximum_maximum_fusion.1), channel_id=1, source_target_pairs={{0,512},{512,0},{1,513},{513,1},{2,514},{514,2},{3,515},{515,3},{4... | collective-permute-start | bytes 193544 | tf_op jit(solution)/shard_map/ppermute | solution.py:27
  75.6 14.7 %all-to-all-start.2 = ((bf16[8,24,896]{2,1,0:T(8,128)(2,1)}), bf16[8,24,896]{2,1,0:T(8,128)(2,1)S(1)}, u32[]{:S(2)}, u32[]{:S(2)}) async-start(bf16[8,24,896]{2,1,0:T(8,128)(2,1)} %broadcast_in_dim.15), calls=%async_computation.2 | async-start | bytes 688128 | tf_op jit(solution)/shard_map/all_to_all | solution.py:19
  79.1 23.7 %collective-permute-start.4 = (bf16[192,1024]{1,0:T(8,128)(2,1)S(1)}, bf16[192,1024]{1,0:T(8,128)(2,1)S(1)}, u32[]{:S(2)}, u32[]{:S(2)}) collective-permute-start(bf16[192,1024]{1,0:T(8,128)(2,1)S(1)} %copy-done.1), channel_id=1, source_target_pairs={{0,1},{1,0},{2,3},{3,2},{4,5},{5,4},{6,7},{7,6},{8,9},{9,8},{10,11... | collective-permute-start | bytes 1179656 | tf_op jit(solution)/shard_map/ppermute | solution.py:27
  91.9 18.1 %all-to-all-start.3 = ((bf16[32,3,2,1024]{3,2,1,0:T(2,128)(2,1)}), bf16[32,3,2,1024]{3,2,1,0:T(2,128)(2,1)S(1)}, u32[]{:S(2)}, u32[]{:S(2)}) async-start(bf16[32,3,2,1024]{3,2,1,0:T(2,128)(2,1)} %reshape.78), calls=%async_computation.3 | async-start | bytes 786432 | tf_op jit(solution)/shard_map/all_to_all | solution.py:19
  97.6 4.5 %collective-permute-start.3 = (bf16[12,416]{1,0:T(8,128)(2,1)S(1)}, bf16[12,416]{1,0:T(8,128)(2,1)S(1)}, u32[]{:S(2)}, u32[]{:S(2)}) collective-permute-start(bf16[12,416]{1,0:T(8,128)(2,1)S(1)} %slice.50), channel_id=1, source_target_pairs={{0,1},{1,0},{2,3},{3,2},{4,5},{5,4},{6,7},{7,6},{8,9},{9,8},{10,11... | collective-permute-start | bytes 29960 | tf_op jit(solution)/shard_map/ppermute | solution.py:27
  99.6 3.5 %collective-permute-start.5 = (bf16[192,416]{1,0:T(8,128)(2,1)S(1)}, bf16[192,416]{1,0:T(8,128)(2,1)S(1)}, u32[]{:S(2)}, u32[]{:S(2)}) collective-permute-start(bf16[192,416]{1,0:T(8,128)(2,1)S(1)} %get-tuple-element.4), channel_id=1, source_target_pairs={{0,1},{1,0},{2,3},{3,2},{4,5},{5,4},{6,7},{7,6},{8,9},{9,8},{10,11... | collective-permute-start | bytes 479240 | tf_op jit(solution)/shard_map/ppermute | solution.py:27

commit v4 on v3

--- a/solution.py
+++ b/solution.py
@@ -52,12 +52,13 @@
 
     part = lax.dot_general(x, both, (((1,), (1,)), ((), ())), preferred_element_type=F32)
     pieces = exchange(part.astype(BF).reshape(depth, 2 * mine, -1), "z")
-    other_x = swapped(x)
     partial = jnp.sum(pieces.astype(F32), axis=0).astype(BF)
     other = swapped(jnp.concatenate([partial, up], 0), "yh")
+    other_x = swapped(x)
+    first = half == 0
     far = other[2 * mine :]
     pre = partial.astype(F32) + other[: 2 * mine].astype(F32)
-    up = jnp.concatenate([jnp.where(half == 0, up, far), jnp.where(half == 0, far, up)], 0)
+    up = jnp.concatenate([jnp.where(first, up, far), jnp.where(first, far, up)], 0)
 
     cdf = 0.5 * (1.0 + jax.scipy.special.erf(pre * (1.0 / math.sqrt(2.0))))
     slope = cdf + pre * jnp.exp(-0.5 * pre * pre) * (1.0 / math.sqrt(2.0 * math.pi))
@@ -67,7 +68,7 @@
     term = lax.dot_general(gathered, both, (((1,), (0,)), ((), ())), preferred_element_type=F32)
     dx = exchange(term.astype(BF).reshape(chips, micro, own, width), CHIP)
     act = pre * cdf
-    act = jnp.where(half == 0, act[:mine], act[mine:]).astype(BF)
+    act = jnp.where(first, act[:mine], act[mine:]).astype(BF)
     other_act = swapped(act[:, hidden : 2 * hidden])
 
     other_gated = swapped(gathered[:, hidden : 2 * hidden])

time: 112 us -> 112 us (level)
  no operation moved by 1% of the time
where the time goes in v4:
time: 112 us; the launch traced here: 111 us
  starting transfers between devices  51.6 us (46%)
  waiting for transfers between devices  46 us (41%)
  local copies, waits for them, and re-layouts  5.22 us (5%)
  matrix products  3.96 us (4%)
  other arithmetic  3.27 us (3%)
    all_to_all x4, waiting for transfers between devices, exchange(): return lax.all_to_all(pieces, axis, split_axis=0, concat_axis=0, tiled=True)  40.3 us
    all_to_all x4, starting transfers between devices, exchange(): return lax.all_to_all(pieces, axis, split_axis=0, concat_axis=0, tiled=True)  36 us
    ppermute x6, starting transfers between devices, swapped(): return lax.ppermute(value, axis, SWAP)  15.6 us
    ppermute x6, waiting for transfers between devices, swapped(): return lax.ppermute(value, axis, SWAP)  5.67 us
  transfers between devices with their start and end apart: 10, of which 6 were waited for; matrix products, arithmetic and copies ran while one was open for 6% of the time, Pallas kernels for 0%

profile of v4, /device:TPU:18, one launch (start us, length us, event | category | flops | bytes accessed | tf_op | source)
XLA Modules:
  0.0 110.9 jit_solution(4293757273408787107)
XLA Ops:
  0.6 1.6 %convert_bitcast_fusion = bf16[416,1024]{1,0:T(8,128)(2,1)S(1)} fusion(f32[1024,416]{0,1:T(8,128)} %param.4), kind=kLoop, calls=%fused_computation.4 | loop fusion | flops 425984 | bytes 2555904 | tf_op jit(solution)/shard_map/convert_element_type | solution.py:43
  2.2 1.9 %collective-permute-start = (bf16[416,1024]{1,0:T(8,128)(2,1)S(1)}, bf16[416,1024]{1,0:T(8,128)(2,1)S(1)}, u32[]{:S(2)}, u32[]{:S(2)}) collective-permute-start(bf16[416,1024]{1,0:T(8,128)(2,1)S(1)} %convert_bitcast_fusion), channel_id=1, source_target_pairs={{0,1},{1,0},{2,3},{3,2},{4,5},{5,4},{6,7},{7,6},{8,9},{9,8},{10,11... | collective-permute-start | bytes 2555912 | tf_op jit(solution)/shard_map/ppermute | solution.py:27
  4.2 1.0 broadcast_in_dim.13
  5.1 16.5 %all-to-all-start = ((bf16[32,3,2,1024]{3,2,1,0:T(2,128)(2,1)}), bf16[32,3,2,1024]{3,2,1,0:T(2,128)(2,1)S(1)}, u32[]{:S(2)}, u32[]{:S(2)}) async-start(bf16[32,3,2,1024]{3,2,1,0:T(2,128)(2,1)} %broadcast_in_dim.13), calls=%async_computation | async-start | bytes 786432 | tf_op jit(solution)/shard_map/all_to_all | solution.py:19
  21.7 15.8 %all-to-all-done = bf16[32,3,2,1024]{3,2,1,0:T(2,128)(2,1)S(1)} async-done(((bf16[32,3,2,1024]{3,2,1,0:T(2,128)(2,1)}), bf16[32,3,2,1024]{3,2,1,0:T(2,128)(2,1)S(1)}, u32[]{:S(2)}, u32[]{:S(2)}) %all-to-all-start) | async-done | bytes 393248 | tf_op jit(solution)/shard_map/all_to_all | solution.py:19
  37.5 0.9 reshape.73
  38.4 0.3 maximum_maximum_fusion
  38.8 0.6 copy-done
  39.4 1.5 %convolution_convert_fusion.1 = bf16[896,192]{0,1:T(8,128)(2,1)} fusion(bf16[896,1024]{1,0:T(8,128)(2,1)S(1)} %maximum_maximum_fusion, bf16[192,1024]{1,0:T(8,128)(2,1)S(1)} %copy-done), kind=kOutput, calls=%fused_computation.3 | convolution fusion | flops 352493568 | bytes 2572288 | tf_op jit(solution)/shard_map/dot_general | solution.py:53
  41.0 10.5 %all-to-all-start.1 = ((bf16[8,24,896]{2,1,0:T(8,128)(2,1)}), bf16[8,24,896]{2,1,0:T(8,128)(2,1)S(1)}, u32[]{:S(2)}, u32[]{:S(2)}) async-start(bf16[8,24,896]{2,1,0:T(8,128)(2,1)} %bitcast.2), calls=%async_computation.1 | async-start | bytes 688128 | tf_op jit(solution)/shard_map/all_to_all | solution.py:19
  51.6 1.9 %collective-permute-start.1 = (bf16[12,416]{1,0:T(8,128)(2,1)S(1)}, bf16[12,416]{1,0:T(8,128)(2,1)S(1)}, u32[]{:S(2)}, u32[]{:S(2)}) collective-permute-start(bf16[12,416]{1,0:T(8,128)(2,1)S(1)} %select_n.74), channel_id=1, source_target_pairs={{0,1},{1,0},{2,3},{3,2},{4,5},{5,4},{6,7},{7,6},{8,9},{9,8},{10,11... | collective-permute-start | bytes 29960 | tf_op jit(solution)/shard_map/ppermute | solution.py:27
  53.5 10.2 %all-to-all-done.1 = bf16[8,24,896]{2,1,0:T(8,128)(2,1)S(1)} async-done(((bf16[8,24,896]{2,1,0:T(8,128)(2,1)}), bf16[8,24,896]{2,1,0:T(8,128)(2,1)S(1)}, u32[]{:S(2)}, u32[]{:S(2)}) %all-to-all-start.1) | async-done | bytes 344096 | tf_op jit(solution)/shard_map/all_to_all | solution.py:19
  63.8 0.1 maximum_maximum_fusion.1
  63.8 5.5 %collective-permute-start.2 = (bf16[36,896]{1,0:T(8,128)(2,1)S(1)}, bf16[36,896]{1,0:T(8,128)(2,1)S(1)}, u32[]{:S(2)}, u32[]{:S(2)}) collective-permute-start(bf16[36,896]{1,0:T(8,128)(2,1)S(1)} %maximum_maximum_fusion.1), channel_id=1, source_target_pairs={{0,512},{512,0},{1,513},{513,1},{2,514},{514,2},{3,515},{515,3},{4... | collective-permute-start | bytes 193544 | tf_op jit(solution)/shard_map/ppermute | solution.py:27
  69.3 5.4 %collective-permute-done.2 = bf16[36,896]{1,0:T(8,128)(2,1)S(1)} collective-permute-done((bf16[36,896]{1,0:T(8,128)(2,1)S(1)}, bf16[36,896]{1,0:T(8,128)(2,1)S(1)}, u32[]{:S(2)}, u32[]{:S(2)}) %collective-permute-start.2) | collective-permute-done | bytes 64544 | tf_op jit(solution)/shard_map/ppermute | solution.py:27
  74.7 0.1 broadcast_select_fusion.1
  74.9 0.8 broadcast_in_dim.15
  75.6 3.4 %all-to-all-start.2 = ((bf16[8,24,896]{2,1,0:T(8,128)(2,1)}), bf16[8,24,896]{2,1,0:T(8,128)(2,1)S(1)}, u32[]{:S(2)}, u32[]{:S(2)}) async-start(bf16[8,24,896]{2,1,0:T(8,128)(2,1)} %broadcast_in_dim.15), calls=%async_computation.2 | async-start | bytes 688128 | tf_op jit(solution)/shard_map/all_to_all | solution.py:19
  79.1 1.9 %collective-permute-start.4 = (bf16[192,1024]{1,0:T(8,128)(2,1)S(1)}, bf16[192,1024]{1,0:T(8,128)(2,1)S(1)}, u32[]{:S(2)}, u32[]{:S(2)}) collective-permute-start(bf16[192,1024]{1,0:T(8,128)(2,1)S(1)} %copy-done.1), channel_id=1, source_target_pairs={{0,1},{1,0},{2,3},{3,2},{4,5},{5,4},{6,7},{7,6},{8,9},{9,8},{10,11... | collective-permute-start | bytes 1179656 | tf_op jit(solution)/shard_map/ppermute | solution.py:27
  81.1 9.3 %all-to-all-done.2 = bf16[8,24,896]{2,1,0:T(8,128)(2,1)S(1)} async-done(((bf16[8,24,896]{2,1,0:T(8,128)(2,1)}), bf16[8,24,896]{2,1,0:T(8,128)(2,1)S(1)}, u32[]{:S(2)}, u32[]{:S(2)}) %all-to-all-start.2) | async-done | bytes 344096 | tf_op jit(solution)/shard_map/all_to_all | solution.py:19
  90.4 0.6 convolution_convert_fusion
  90.9 0.9 reshape.78
  91.9 5.6 %all-to-all-start.3 = ((bf16[32,3,2,1024]{3,2,1,0:T(2,128)(2,1)}), bf16[32,3,2,1024]{3,2,1,0:T(2,128)(2,1)S(1)}, u32[]{:S(2)}, u32[]{:S(2)}) async-start(bf16[32,3,2,1024]{3,2,1,0:T(2,128)(2,1)} %reshape.78), calls=%async_computation.3 | async-start | bytes 786432 | tf_op jit(solution)/shard_map/all_to_all | solution.py:19
  97.5 0.1 slice.50
  97.6 1.9 %collective-permute-start.3 = (bf16[12,416]{1,0:T(8,128)(2,1)S(1)}, bf16[12,416]{1,0:T(8,128)(2,1)S(1)}, u32[]{:S(2)}, u32[]{:S(2)}) collective-permute-start(bf16[12,416]{1,0:T(8,128)(2,1)S(1)} %slice.50), channel_id=1, source_target_pairs={{0,1},{1,0},{2,3},{3,2},{4,5},{5,4},{6,7},{7,6},{8,9},{9,8},{10,11... | collective-permute-start | bytes 29960 | tf_op jit(solution)/shard_map/ppermute | solution.py:27
  99.5 0.1 fusion.15
  99.6 2.4 %collective-permute-start.5 = (bf16[192,416]{1,0:T(8,128)(2,1)S(1)}, bf16[192,416]{1,0:T(8,128)(2,1)S(1)}, u32[]{:S(2)}, u32[]{:S(2)}) collective-permute-start(bf16[192,416]{1,0:T(8,128)(2,1)S(1)} %get-tuple-element.4), channel_id=1, source_target_pairs={{0,1},{1,0},{2,3},{3,2},{4,5},{5,4},{6,7},{7,6},{8,9},{9,8},{10,11... | collective-permute-start | bytes 479240 | tf_op jit(solution)/shard_map/ppermute | solution.py:27
  102.2 0.6 reshape.76
  102.8 0.3 collective-permute-done.5
  103.1 1.8 %convolution_multiply_fusion = f32[1024,416]{0,1:T(8,128)} fusion(bf16[192,1024]{1,0:T(8,128)(2,1)S(1)} %collective-permute-done.4, bf16[192,1024]{1,0:T(8,128)(2,1)S(1)} %copy-done.1, bf16[192,416]{1,0:T(8,128)(2,1)S(1)} %collective-permute-done.5, bf16[192,416]{1,0:T(8,128)(2,1)S(1)} %get-tuple-element.3), kind=kOutput, calls=%fused_computation.1 | convolution fusion | flops 329793536 | bytes 2809856 | tf_op jit(solution)/shard_map/dot_general | solution.py:77
  104.9 5.0 %all-to-all-done.3 = bf16[32,3,2,1024]{3,2,1,0:T(2,128)(2,1)S(1)} async-done(((bf16[32,3,2,1024]{3,2,1,0:T(2,128)(2,1)}), bf16[32,3,2,1024]{3,2,1,0:T(2,128)(2,1)S(1)}, u32[]{:S(2)}, u32[]{:S(2)}) %all-to-all-start.3) | async-done | bytes 393248 | tf_op jit(solution)/shard_map/all_to_all | solution.py:19
  109.9 0.9 reduce_sum.25
  (28 shorter events, 0.5 us)
Async XLA Ops:
  0.6 3.5 %copy-start.3 = (bf16[3,2,1024]{2,1,0:T(2,128)(2,1)S(1)}, bf16[3,2,1024]{2,1,0:T(2,128)(2,1)}, u32[]{:S(2)}) copy-start(bf16[3,2,1024]{2,1,0:T(2,128)(2,1)} %param.3) | copy-start | bytes 36868
  2.2 36.2 %collective-permute-start = (bf16[416,1024]{1,0:T(8,128)(2,1)S(1)}, bf16[416,1024]{1,0:T(8,128)(2,1)S(1)}, u32[]{:S(2)}, u32[]{:S(2)}) collective-permute-start(bf16[416,1024]{1,0:T(8,128)(2,1)S(1)} %convert_bitcast_fusion), channel_id=1, source_target_pairs={{0,1},{1,0},{2,3},{3,2},{4,5},{5,4},{6,7},{7,6},{8,9},{9,8},{10,11... | collective-permute-start | bytes 2555912 | tf_op jit(solution)/shard_map/ppermute | solution.py:27
  5.1 32.4 %all-to-all-start = ((bf16[32,3,2,1024]{3,2,1,0:T(2,128)(2,1)}), bf16[32,3,2,1024]{3,2,1,0:T(2,128)(2,1)S(1)}, u32[]{:S(2)}, u32[]{:S(2)}) async-start(bf16[32,3,2,1024]{3,2,1,0:T(2,128)(2,1)} %broadcast_in_dim.13), calls=%async_computation | async-start | bytes 786432 | tf_op jit(solution)/shard_map/all_to_all | solution.py:19
  38.4 1.0 copy-start
  39.4 12.0 %copy-start.2 = (bf16[3,8,416]{2,1,0:T(8,128)(2,1)S(1)}, bf16[3,8,416]{2,1,0:T(8,128)(2,1)}, u32[]{:S(2)}) copy-start(bf16[3,8,416]{2,1,0:T(8,128)(2,1)} %param.5) | copy-start | bytes 59908
  41.0 38.1 %copy-start.1 = (bf16[192,1024]{1,0:T(8,128)(2,1)S(1)}, bf16[192,1024]{1,0:T(8,128)(2,1)}, u32[]{:S(2)}) copy-start(bf16[192,1024]{1,0:T(8,128)(2,1)} %reshape.73) | copy-start | bytes 1179652
  41.0 22.7 %all-to-all-start.1 = ((bf16[8,24,896]{2,1,0:T(8,128)(2,1)}), bf16[8,24,896]{2,1,0:T(8,128)(2,1)S(1)}, u32[]{:S(2)}, u32[]{:S(2)}) async-start(bf16[8,24,896]{2,1,0:T(8,128)(2,1)} %bitcast.2), calls=%async_computation.1 | async-start | bytes 688128 | tf_op jit(solution)/shard_map/all_to_all | solution.py:19
  51.6 12.2 %collective-permute-start.1 = (bf16[12,416]{1,0:T(8,128)(2,1)S(1)}, bf16[12,416]{1,0:T(8,128)(2,1)S(1)}, u32[]{:S(2)}, u32[]{:S(2)}) collective-permute-start(bf16[12,416]{1,0:T(8,128)(2,1)S(1)} %select_n.74), channel_id=1, source_target_pairs={{0,1},{1,0},{2,3},{3,2},{4,5},{5,4},{6,7},{7,6},{8,9},{9,8},{10,11... | collective-permute-start | bytes 29960 | tf_op jit(solution)/shard_map/ppermute | solution.py:27
  63.8 10.9 %collective-permute-start.2 = (bf16[36,896]{1,0:T(8,128)(2,1)S(1)}, bf16[36,896]{1,0:T(8,128)(2,1)S(1)}, u32[]{:S(2)}, u32[]{:S(2)}) collective-permute-start(bf16[36,896]{1,0:T(8,128)(2,1)S(1)} %maximum_maximum_fusion.1), channel_id=1, source_target_pairs={{0,512},{512,0},{1,513},{513,1},{2,514},{514,2},{3,515},{515,3},{4... | collective-permute-start | bytes 193544 | tf_op jit(solution)/shard_map/ppermute | solution.py:27
  75.6 14.7 %all-to-all-start.2 = ((bf16[8,24,896]{2,1,0:T(8,128)(2,1)}), bf16[8,24,896]{2,1,0:T(8,128)(2,1)S(1)}, u32[]{:S(2)}, u32[]{:S(2)}) async-start(bf16[8,24,896]{2,1,0:T(8,128)(2,1)} %broadcast_in_dim.15), calls=%async_computation.2 | async-start | bytes 688128 | tf_op jit(solution)/shard_map/all_to_all | solution.py:19
  79.1 23.7 %collective-permute-start.4 = (bf16[192,1024]{1,0:T(8,128)(2,1)S(1)}, bf16[192,1024]{1,0:T(8,128)(2,1)S(1)}, u32[]{:S(2)}, u32[]{:S(2)}) collective-permute-start(bf16[192,1024]{1,0:T(8,128)(2,1)S(1)} %copy-done.1), channel_id=1, source_target_pairs={{0,1},{1,0},{2,3},{3,2},{4,5},{5,4},{6,7},{7,6},{8,9},{9,8},{10,11... | collective-permute-start | bytes 1179656 | tf_op jit(solution)/shard_map/ppermute | solution.py:27
  91.9 18.1 %all-to-all-start.3 = ((bf16[32,3,2,1024]{3,2,1,0:T(2,128)(2,1)}), bf16[32,3,2,1024]{3,2,1,0:T(2,128)(2,1)S(1)}, u32[]{:S(2)}, u32[]{:S(2)}) async-start(bf16[32,3,2,1024]{3,2,1,0:T(2,128)(2,1)} %reshape.78), calls=%async_computation.3 | async-start | bytes 786432 | tf_op jit(solution)/shard_map/all_to_all | solution.py:19
  97.6 4.5 %collective-permute-start.3 = (bf16[12,416]{1,0:T(8,128)(2,1)S(1)}, bf16[12,416]{1,0:T(8,128)(2,1)S(1)}, u32[]{:S(2)}, u32[]{:S(2)}) collective-permute-start(bf16[12,416]{1,0:T(8,128)(2,1)S(1)} %slice.50), channel_id=1, source_target_pairs={{0,1},{1,0},{2,3},{3,2},{4,5},{5,4},{6,7},{7,6},{8,9},{9,8},{10,11... | collective-permute-start | bytes 29960 | tf_op jit(solution)/shard_map/ppermute | solution.py:27
  99.6 3.5 %collective-permute-start.5 = (bf16[192,416]{1,0:T(8,128)(2,1)S(1)}, bf16[192,416]{1,0:T(8,128)(2,1)S(1)}, u32[]{:S(2)}, u32[]{:S(2)}) collective-permute-start(bf16[192,416]{1,0:T(8,128)(2,1)S(1)} %get-tuple-element.4), channel_id=1, source_target_pairs={{0,1},{1,0},{2,3},{3,2},{4,5},{5,4},{6,7},{7,6},{8,9},{9,8},{10,11... | collective-permute-start | bytes 479240 | tf_op jit(solution)/shard_map/ppermute | solution.py:27
